TPU v7x, 32 devices: a whole 2x2x4 slice. The times are simulated.
32 devices in a mesh: parts: 2 (over y), users: 16 (over z, x, core).
Axes of the slice: x: 2, y: 2, z: 4, core: 2. Of those that a mesh axis runs over, the one named last changes fastest.
Arguments:
- candidates: bfloat16 [512, 512], P(('parts', 'users')), parts along dimension 0, may hold values from -6 to 6
- candidate_user: int32 [512], P(('parts', 'users')), parts along dimension 0, may hold values from 0 to 7
- events: bfloat16 [65536, 512], P(('parts', 'users')), parts along dimension 0, may hold values from -6 to 6
- event_user: int32 [65536], P(('parts', 'users')), parts along dimension 0, may hold values from 0 to 7, never falling along the last dimension, each value on 1 to 12288 neighbouring positions
- event_mask: int32 [65536], P(('parts', 'users')), parts along dimension 0, may hold values 0 or 1
- query_weight: bfloat16 [512, 512], replicated, may hold values from -0.25 to 0.25
- key_weight: bfloat16 [512, 512], replicated, may hold values from -0.25 to 0.25
- value_weight: bfloat16 [512, 512], replicated, may hold values from -2 to 2
- gate_weight: bfloat16 [512, 512], replicated, may hold values from -0.25 to 0.25
- output_weight: bfloat16 [512, 512], replicated, may hold values from -0.25 to 0.25
Outputs:
- candidate_out: bfloat16 [512, 512], P(('parts', 'users')), parts along dimension 0
There are 2 independent parts, one for each index of `parts`. A program takes and returns all parts, laid end to end along the dimension named above; an argument that names none is the same for every part. Nothing has to cross between parts.
Inputs may be any that keep to these rules, and one draw needn't show every extreme that they name: event_user never falls along the events; each user's events form one run of at most 12288 slots.
All inputs are finite; a program needn't handle non-finite values. No bound on the sum of `event_mask` on one device may be relied on, other than what follows from the above.
Results may differ from a plain program's by a relative error of at most 0.0044.
Values may be sent and summed in bfloat16 or wider, within the bound.
No kernel may reach another device: no remote copies, remote signals or barrier semaphores. Data moves between devices by JAX's collectives and lax.ppermute only.
A program may use at most 64 MiB of HBM per device.

v0:
```python
import math
import jax
import jax.numpy as jnp
from jax import lax
from jax.sharding import PartitionSpec as P

HEADS = 4


def per_device(
    candidates,
    candidate_user,
    events,
    event_user,
    event_mask,
    query_weight,
    key_weight,
    value_weight,
    gate_weight,
    output_weight,
):
    own_count = candidates.shape[0]
    model_width = candidates.shape[1]
    head_count = HEADS
    head_size = model_width // head_count
    score_scale = 1.0 / math.sqrt(head_size)
    queries = jnp.dot(candidates, query_weight, preferred_element_type=jnp.float32).astype(
        jnp.bfloat16
    )
    gate_values = jax.nn.silu(jnp.dot(candidates, gate_weight, preferred_element_type=jnp.float32))
    key_rows = jnp.dot(events, key_weight, preferred_element_type=jnp.float32).astype(jnp.bfloat16)
    value_rows = jnp.dot(events, value_weight, preferred_element_type=jnp.float32).astype(
        jnp.bfloat16
    )
    event_count = key_rows.shape[0]
    key_heads = key_rows.reshape(event_count, head_count, head_size)
    value_heads = value_rows.reshape(event_count, head_count, head_size)
    valid_events = event_mask.astype(jnp.float32)
    all_queries, all_users = (
        lax.all_gather(queries, "users", axis=0, tiled=True),
        lax.all_gather(candidate_user, "users", axis=0, tiled=True),
    )

    def one_block(block_pair):
        query_block, user_block = block_pair
        scores = (
            jnp.einsum("chd,ehd->hce", query_block, key_heads, preferred_element_type=jnp.float32)
            * score_scale
        )
        same_user = (user_block[:, None] == event_user[None, :]).astype(jnp.float32) * valid_events[
            None, :
        ]
        attn_weights = (jax.nn.silu(scores) * same_user[None]).astype(jnp.bfloat16)
        mixed_rows = jnp.einsum(
            "hce,ehd->chd", attn_weights, value_heads, preferred_element_type=jnp.float32
        )
        return mixed_rows.reshape(query_block.shape[0], model_width)

    row_count = own_count * lax.axis_size("users")
    row_block = math.gcd(row_count, 512)
    query_part = all_queries
    query_part = query_part.reshape(row_count // row_block, row_block, head_count, head_size)
    user_part = all_users.reshape(row_count // row_block, row_block)
    summed = lax.psum_scatter(
        lax.map(one_block, (query_part, user_part)).reshape(row_count, model_width),
        "users",
        scatter_dimension=0,
        tiled=True,
    )
    mean_row = jnp.mean(summed, axis=1, keepdims=True)
    centred = summed - mean_row
    var_row = jnp.mean(centred * centred, axis=1, keepdims=True)
    normed = centred / jnp.sqrt(var_row + 1e-05)
    gated_rows = (normed * gate_values).astype(jnp.bfloat16)
    result = candidates.astype(jnp.float32) + jnp.dot(
        gated_rows, output_weight, preferred_element_type=jnp.float32
    )
    return result.astype(jnp.bfloat16)


def solution(mesh):
    in_specs = (
        P(("parts", "users"), None),
        P(("parts", "users")),
        P(("parts", "users"), None),
        P(("parts", "users")),
        P(("parts", "users")),
        P(),
        P(),
        P(),
        P(),
        P(),
    )
    out_specs = P(("parts", "users"), None)
    return jax.shard_map(
        per_device, mesh=mesh, in_specs=in_specs, out_specs=out_specs, check_vma=False
    )
```

profile of v0, /device:TPU:0, one launch (start us, length us, event | category | flops | bytes accessed | tf_op | source)
XLA Modules:
  0.0 126.6 jit_solution(15532757817765731174)
XLA Ops:
  6.5 0.0 copy-start
  6.5 0.0 reduce-scatter.2.cloned.1.call-start
  6.5 1.4 %dynamic-slice.1 = u32[1]{0:T(128)} dynamic-slice(u32[32]{0:T(128)} %constant.34, u32[]{:T(128)S(6)} %add.28), dynamic_slice_sizes={1} | dynamic-slice | bytes 12
  8.6 0.9 dynamic-update-slice
  9.4 13.7 %all-reduce = s32[256]{0:T(256)S(1)} all-reduce(s32[256]{0:T(256)S(1)} %dynamic-update-slice), channel_id=1, replica_groups=mesh['parts'=2,'users'=16] {'users'}, use_global_device_ids=true, to_apply=%add | all-reduce | flops 256 | bytes 2048
  23.2 0.7 convert_element_type.31
  23.9 1.2 convolution_convert_fusion.2
  25.1 18.7 %all_gather.6 = bf16[256,512]{1,0:T(8,128)(2,1)S(1)} all-gather(bf16[16,512]{1,0:T(8,128)(2,1)S(1)} %convolution_convert_fusion.2), channel_id=1, replica_groups=mesh['parts'=2,'users'=16] {'users'}, dimensions={0}, use_global_device_ids=true | all-gather | bytes 278528 | tf_op jit(solution)/shard_map/all_gather | solution.py:40
  43.8 0.0 copy-done
  43.8 0.0 copy-start.5
  43.8 3.7 %convolution_convert_fusion = bf16[2048,512]{0,1:T(8,128)(2,1)} fusion(bf16[2048,512]{1,0:T(8,128)(2,1)S(1)} %copy-done, bf16[512,512]{1,0:T(8,128)(2,1)} %param.16), kind=kOutput, calls=%fused_computation.1 | convolution fusion | flops 1074790400 | bytes 4718592 | tf_op jit(solution)/shard_map/dot_general | solution.py:31
  47.5 0.0 copy-done.5
  47.5 0.0 copy-start.4
  47.5 2.7 %convolution_convert_fusion.1 = bf16[2048,512]{0,1:T(8,128)(2,1)} fusion(bf16[2048,512]{1,0:T(8,128)(2,1)S(1)} %copy-done, bf16[512,512]{1,0:T(8,128)(2,1)S(1)} %copy-done.5), kind=kOutput, calls=%fused_computation.2 | convolution fusion | flops 1074790400 | bytes 4718592 | tf_op jit(solution)/shard_map/dot_general | solution.py:32
  50.1 0.0 copy-done.4
  50.1 1.5 %compare_select_fusion = f32[256,2048]{1,0:T(8,128)} fusion(f32[2048]{0:T(1024)S(1)} %convert_element_type.31, s32[2048]{0:T(1024)S(1)} %copy-done.4, s32[256]{0:T(256)S(1)} %all-reduce), kind=kLoop, calls=%fused_computation.3 | loop fusion | flops 1048576 | bytes 2114560 | tf_op jit(solution)/shard_map/while/body/eval_jaxpr/mul | solution.py:50
  51.7 0.0 copy-start.1
  51.7 0.0 copy-start.2
  51.7 0.0 copy-start.3
  51.7 8.2 %fusion = f32[4,128,256]{2,1,0:T(8,128)} fusion(bf16[2048,4,128]{0,2,1:T(8,128)(2,1)} %bitcast.28, bf16[2048,4,128]{0,2,1:T(8,128)(2,1)} %bitcast.27, f32[256,2048]{1,0:T(8,128)} %compare_select_fusion, bf16[256,512]{1,0:T(8,128)(2,1)S(1)} %all_gather.6), kind=kOutput, calls=%fused_computation.4 | convolution fusion | flops 1088421888 | bytes 7077888 | tf_op jit(solution)/shard_map/while/body/eval_jaxpr/hce,ehd->chd/dot_general | solution.py:54
  59.9 2.0 %copy.13 = f32[256,512]{1,0:T(8,128)} copy(f32[256,512]{0,1:T(8,128)} %bitcast.26) | data formatting | bytes 1048576 | tf_op jit(solution)/shard_map/reshape | solution.py:65
  61.9 0.0 reduce-scatter.2.cloned.1.call-update
  61.9 54.3 %reduce-scatter.2.cloned.1.call-done = f32[16,512]{1,0:T(8,128)} async-done(((f32[256,512]{1,0:T(8,128)}), f32[16,512]{1,0:T(8,128)}) %reduce-scatter.2.cloned.1.call-update) | async-done | bytes 32784 | tf_op jit(solution)/shard_map/reduce_scatter | solution.py:64
  116.2 0.9 reduce_sum.18
  117.1 0.9 multiply_reduce_fusion
  118.0 0.0 copy-done.1
  118.0 0.0 copy-done.2
  118.1 0.0 copy-done.3
  118.1 1.7 %fusion.1 = bf16[16,512]{1,0:T(8,128)(2,1)} fusion(bf16[512,512]{1,0:T(8,128)(2,1)S(1)} %copy-done.1, bf16[16,512]{1,0:T(8,128)(2,1)S(1)} %copy-done.3, f32[16,512]{1,0:T(8,128)} %reduce-scatter.2.cloned.1.call-done, f32[16]{0:T(128)S(1)} %add_sqrt_fusion, f32[16]{0:T(128)S(1)} %broadcast_multiply_fusion, bf16[512,512]{1,0:T(8,128)(2,1)S(1)} %copy-done.2), kind=kOutput, calls=%fused_computation.6 | convolution fusion | flops 16867328 | bytes 1114240 | tf_op jit(solution)/shard_map/dot_general | solution.py:75
  (3 shorter events, 0.0 us)
Async XLA Ops:
  6.5 37.2 %copy-start = (bf16[2048,512]{1,0:T(8,128)(2,1)S(1)}, bf16[2048,512]{1,0:T(8,128)(2,1)}, u32[]{:S(2)}) copy-start(bf16[2048,512]{1,0:T(8,128)(2,1)} %param.12) | copy-start | bytes 6291460
  6.5 109.7 %reduce-scatter.2.cloned.1.call-start = ((), (), s32[]{:S(2)}) async-start(), calls=%async_computation.1 | async-start | bytes 557056 | tf_op jit(solution)/shard_map/reduce_scatter | solution.py:64
  43.8 3.7 %copy-start.5 = (bf16[512,512]{1,0:T(8,128)(2,1)S(1)}, bf16[512,512]{1,0:T(8,128)(2,1)}, u32[]{:S(2)}) copy-start(bf16[512,512]{1,0:T(8,128)(2,1)} %param.17) | copy-start | bytes 1572868
  47.5 2.7 %copy-start.4 = (s32[2048]{0:T(1024)S(1)}, s32[2048]{0:T(1024)}, u32[]{:S(2)}) copy-start(s32[2048]{0:T(1024)} %param.13) | copy-start | bytes 24580
  51.7 66.4 %copy-start.1 = (bf16[512,512]{1,0:T(8,128)(2,1)S(1)}, bf16[512,512]{1,0:T(8,128)(2,1)}, u32[]{:S(2)}) copy-start(bf16[512,512]{1,0:T(8,128)(2,1)} %param.19) | copy-start | bytes 1572868
  51.7 66.4 %copy-start.2 = (bf16[512,512]{1,0:T(8,128)(2,1)S(1)}, bf16[512,512]{1,0:T(8,128)(2,1)}, u32[]{:S(2)}) copy-start(bf16[512,512]{1,0:T(8,128)(2,1)} %param.18) | copy-start | bytes 1572868
  51.7 66.4 %copy-start.3 = (bf16[16,512]{1,0:T(8,128)(2,1)S(1)}, bf16[16,512]{1,0:T(8,128)(2,1)}, u32[]{:S(2)}) copy-start(bf16[16,512]{1,0:T(8,128)(2,1)} %param.10) | copy-start | bytes 49156
Sparse Core Ops, SparseCore 0:
  62.0 54.1 reduce-scatter.1
where the time goes:
time: 127 us
  waiting for transfers between devices  54.3 us (43%)
  blocking collectives  32.4 us (26%)
  matrix products  17.5 us (14%)
  between operations  14.1 us (11%)
  local copies, waits for them, and re-layouts  4.3 us (3%)
  other arithmetic  4.07 us (3%)
    reduce_scatter x1, waiting for transfers between devices, per_device(): lax.psum_scatter(lax.map(one_block, (query_part, user_part)).reshape(row_...  54.3 us
    all_gather x1, blocking collectives, per_device(): lax.all_gather(queries, 'users', axis=0, tiled=True)  18.7 us
    unnamed x1, blocking collectives  13.7 us
    dot_general x1, matrix products, one_block(): jnp.einsum('hce,ehd->chd', attn_weights, value_heads, preferred_element_t...  8.19 us
    dot_general x1, matrix products, per_device(): jnp.dot(events, key_weight, preferred_element_type=jnp.float32)  3.69 us
    dot_general x1, matrix products, per_device(): jnp.dot(events, value_weight, preferred_element_type=jnp.float32)  2.65 us
  transfers between devices with their start and end apart: 1, of which 1 were waited for; matrix products, arithmetic and copies ran while one was open for 0% of the time, Pallas kernels for 0%

commit v1 on v0

--- a/solution.py
+++ b/solution.py
@@ -1,3 +1,4 @@
+import functools
 import math
 import jax
 import jax.numpy as jnp
@@ -5,6 +6,26 @@
 from jax.sharding import PartitionSpec as P
 
 HEADS = 4
+
+
+def save_sides(sample, dim_i):
+    full_n = jax.lax.psum(1, "users")
+    trail = [(j0, (j0 + 1) % full_n) for j0 in range(full_n)]
+    after, state_now = ([sample], [sample])
+    pieces_in = [(j0, (j0 - 1) % full_n) for j0 in range(full_n)]
+    for _ in range(full_n // 2):
+        after.append(jax.lax.ppermute(after[-1], "users", trail))
+    for _ in [*range((full_n - 1) // 2)]:
+        state_now.append(jax.lax.ppermute(state_now[-1], "users", pieces_in))
+    x_new = jnp.roll(
+        jnp.concatenate([*after[::-1], *state_now[1:]], axis=dim_i),
+        (jax.lax.axis_index("users") - full_n // 2) * sample.shape[dim_i],
+        axis=dim_i,
+    )
+    return x_new
+
+
+spot_link = functools.partial(save_sides, dim_i=0)
 
 
 def per_device(
@@ -37,7 +58,7 @@
     value_heads = value_rows.reshape(event_count, head_count, head_size)
     valid_events = event_mask.astype(jnp.float32)
     all_queries, all_users = (
-        lax.all_gather(queries, "users", axis=0, tiled=True),
+        spot_link(queries),
         lax.all_gather(candidate_user, "users", axis=0, tiled=True),
     )
 

time: 127 us -> 150 us (1.18)
  starting transfers between devices: 0.01 us -> 27.2 us
  blocking collectives: 32.4 us -> 12.1 us
  waiting for transfers between devices: 54.3 us -> 69.9 us
    ppermute x0 -> x15, starting transfers between devices: none -> 27.2 us  [the longest x7 26.2 us: save_sides(): state_now.append(jax.lax.ppermute(state_now[-1], 'users', pieces_in))]
    all_gather x1 -> x0, blocking collectives: 18.7 us -> none  [per_device(): lax.all_gather(queries, 'users', axis=0, tiled=True)]
    ppermute x0 -> x15, waiting for transfers between devices: none -> 12 us  [the longest x8 10.6 us: save_sides(): after.append(jax.lax.ppermute(after[-1], 'users', trail))]
    reduce_scatter x1, waiting for transfers between devices: 54.3 us -> 58 us  [per_device(): lax.psum_scatter(lax.map(one_block, (query_part, user_part)).reshape(row_...]
    unnamed x1, blocking collectives: 13.7 us -> 12.1 us
  transfers between devices with their start and end apart: 1 -> 16, of which waited for: 1 -> 6; matrix products, arithmetic and copies ran while one was open for 0% -> 7% of each run, Pallas kernels for 0% -> 0%
where the time goes in v1:
time: 150 us; the launch traced here: 149 us
  waiting for transfers between devices  69.9 us (47%)
  starting transfers between devices  27.2 us (18%)
  matrix products  16.5 us (11%)
  between operations  14.4 us (10%)
  blocking collectives  12.1 us (8%)
  other arithmetic  4.76 us (3%)
  local copies, waits for them, and re-layouts  4.44 us (3%)
    reduce_scatter x1, waiting for transfers between devices, per_device(): lax.psum_scatter(lax.map(one_block, (query_part, user_part)).reshape(row_...  58 us
    ppermute x7, starting transfers between devices, save_sides(): state_now.append(jax.lax.ppermute(state_now[-1], 'users', pieces_in))  26.2 us
    unnamed x1, blocking collectives  12.1 us
    ppermute x8, waiting for transfers between devices, save_sides(): after.append(jax.lax.ppermute(after[-1], 'users', trail))  10.6 us
    dot_general x1, matrix products, one_block(): jnp.einsum('hce,ehd->chd', attn_weights, value_heads, preferred_element_t...  8.14 us
  transfers between devices with their start and end apart: 16, of which 6 were waited for; matrix products, arithmetic and copies ran while one was open for 7% of the time, Pallas kernels for 0%

profile of v1, /device:TPU:0, one launch (start us, length us, event | category | flops | bytes accessed | tf_op | source)
XLA Modules:
  0.0 149.2 jit_solution(16934273846662759990)
XLA Ops:
  6.5 1.4 convolution_convert_fusion.2
  7.9 0.5 collective-permute-start
  8.4 6.4 %collective-permute-done = bf16[16,512]{1,0:T(8,128)(2,1)S(1)} collective-permute-done((bf16[16,512]{1,0:T(8,128)(2,1)S(1)}, bf16[16,512]{1,0:T(8,128)(2,1)S(1)}, u32[]{:S(2)}, u32[]{:S(2)}) %collective-permute-start) | collective-permute-done | bytes 16416 | tf_op jit(solution)/shard_map/ppermute | solution.py:17
  14.8 0.0 collective-permute-start.1
  14.8 4.4 %collective-permute-start.8 = (bf16[16,512]{1,0:T(8,128)(2,1)S(1)}, bf16[16,512]{1,0:T(8,128)(2,1)S(1)}, u32[]{:S(2)}, u32[]{:S(2)}) collective-permute-start(bf16[16,512]{1,0:T(8,128)(2,1)S(1)} %convolution_convert_fusion.2), channel_id=1, source_target_pairs={{0,15},{1,0},{2,1},{3,2},{4,3},{5,4},{6,5},{7,6},{8,7},{9,8},{10,9... | collective-permute-start | bytes 49160 | tf_op jit(solution)/shard_map/ppermute | solution.py:19
  19.2 1.4 collective-permute-done.1
  20.7 0.0 collective-permute-start.2
  20.7 0.0 collective-permute-done.8
  20.7 4.4 %collective-permute-start.9 = (bf16[16,512]{1,0:T(8,128)(2,1)S(1)}, bf16[16,512]{1,0:T(8,128)(2,1)S(1)}, u32[]{:S(2)}, u32[]{:S(2)}) collective-permute-start(bf16[16,512]{1,0:T(8,128)(2,1)S(1)} %collective-permute-done.8), channel_id=1, source_target_pairs={{0,15},{1,0},{2,1},{3,2},{4,3},{5,4},{6,5},{7,6},{8,7},{9,8},{10,9... | collective-permute-start | bytes 49160 | tf_op jit(solution)/shard_map/ppermute | solution.py:19
  25.1 1.4 collective-permute-done.2
  26.5 0.0 collective-permute-start.3
  26.5 0.0 collective-permute-done.9
  26.5 4.4 %collective-permute-start.10 = (bf16[16,512]{1,0:T(8,128)(2,1)S(1)}, bf16[16,512]{1,0:T(8,128)(2,1)S(1)}, u32[]{:S(2)}, u32[]{:S(2)}) collective-permute-start(bf16[16,512]{1,0:T(8,128)(2,1)S(1)} %collective-permute-done.9), channel_id=1, source_target_pairs={{0,15},{1,0},{2,1},{3,2},{4,3},{5,4},{6,5},{7,6},{8,7},{9,8},{10,9... | collective-permute-start | bytes 49160 | tf_op jit(solution)/shard_map/ppermute | solution.py:19
  31.0 1.4 collective-permute-done.3
  32.4 0.0 collective-permute-start.4
  32.4 0.7 convert_element_type.31
  33.1 1.2 dynamic-slice.1
  35.0 0.9 dynamic-update-slice
  35.8 12.1 %all-reduce = s32[256]{0:T(256)S(1)} all-reduce(s32[256]{0:T(256)S(1)} %dynamic-update-slice), channel_id=1, replica_groups=mesh['parts'=2,'users'=16] {'users'}, use_global_device_ids=true, to_apply=%add | all-reduce | flops 256 | bytes 2048
  47.9 0.0 collective-permute-done.10
  47.9 0.0 collective-permute-start.11
  47.9 0.0 collective-permute-done.4
  47.9 0.5 collective-permute-start.5
  48.4 2.2 %compare_select_fusion = f32[256,2048]{1,0:T(8,128)} fusion(f32[2048]{0:T(1024)S(1)} %convert_element_type.31, s32[2048]{0:T(1024)} %param.13, s32[256]{0:T(256)S(1)} %all-reduce), kind=kLoop, calls=%fused_computation.3 | loop fusion | flops 1048576 | bytes 2114560 | tf_op jit(solution)/shard_map/while/body/eval_jaxpr/mul | solution.py:71
  50.7 0.0 collective-permute-done.11
  50.7 4.0 %collective-permute-start.12 = (bf16[16,512]{1,0:T(8,128)(2,1)S(1)}, bf16[16,512]{1,0:T(8,128)(2,1)S(1)}, u32[]{:S(2)}, u32[]{:S(2)}) collective-permute-start(bf16[16,512]{1,0:T(8,128)(2,1)S(1)} %collective-permute-done.11), channel_id=1, source_target_pairs={{0,15},{1,0},{2,1},{3,2},{4,3},{5,4},{6,5},{7,6},{8,7},{9,8},{10,9... | collective-permute-start | bytes 49160 | tf_op jit(solution)/shard_map/ppermute | solution.py:19
  54.7 0.0 collective-permute-done.5
  54.7 0.0 collective-permute-start.6
  54.7 2.6 %convolution_convert_fusion = bf16[2048,512]{0,1:T(8,128)(2,1)} fusion(bf16[2048,512]{1,0:T(8,128)(2,1)S(1)} %copy-done, bf16[512,512]{1,0:T(8,128)(2,1)S(1)} %copy-done.4), kind=kOutput, calls=%fused_computation.1 | convolution fusion | flops 1074790400 | bytes 4718592 | tf_op jit(solution)/shard_map/dot_general | solution.py:52
  57.3 0.0 collective-permute-done.12
  57.3 4.4 %collective-permute-start.13 = (bf16[16,512]{1,0:T(8,128)(2,1)S(1)}, bf16[16,512]{1,0:T(8,128)(2,1)S(1)}, u32[]{:S(2)}, u32[]{:S(2)}) collective-permute-start(bf16[16,512]{1,0:T(8,128)(2,1)S(1)} %collective-permute-done.12), channel_id=1, source_target_pairs={{0,15},{1,0},{2,1},{3,2},{4,3},{5,4},{6,5},{7,6},{8,7},{9,8},{10,9... | collective-permute-start | bytes 49160 | tf_op jit(solution)/shard_map/ppermute | solution.py:19
  61.7 0.0 collective-permute-done.6
  61.7 0.0 collective-permute-start.7
  61.7 2.6 %convolution_convert_fusion.1 = bf16[2048,512]{0,1:T(8,128)(2,1)} fusion(bf16[2048,512]{1,0:T(8,128)(2,1)S(1)} %copy-done, bf16[512,512]{1,0:T(8,128)(2,1)S(1)} %copy-done.5), kind=kOutput, calls=%fused_computation.2 | convolution fusion | flops 1074790400 | bytes 4718592 | tf_op jit(solution)/shard_map/dot_general | solution.py:53
  64.4 0.0 collective-permute-done.13
  64.4 4.4 %collective-permute-start.14 = (bf16[16,512]{1,0:T(8,128)(2,1)S(1)}, bf16[16,512]{1,0:T(8,128)(2,1)S(1)}, u32[]{:S(2)}, u32[]{:S(2)}) collective-permute-start(bf16[16,512]{1,0:T(8,128)(2,1)S(1)} %collective-permute-done.13), channel_id=1, source_target_pairs={{0,15},{1,0},{2,1},{3,2},{4,3},{5,4},{6,5},{7,6},{8,7},{9,8},{10,9... | collective-permute-start | bytes 49160 | tf_op jit(solution)/shard_map/ppermute | solution.py:19
  69.0 1.3 collective-permute-done.14
  70.5 0.1 copy.13
  70.6 0.0 copy-start.1
  70.6 0.0 copy-start.2
  70.6 0.0 copy-start.3
  70.6 8.1 %fusion = f32[4,128,256]{2,1,0:T(8,128)} fusion(bf16[2048,4,128]{0,2,1:T(8,128)(2,1)} %bitcast.22, bf16[256,4,128]{0,2,1:T(8,128)(2,1)S(1)} %bitcast.20, bf16[2048,4,128]{0,2,1:T(8,128)(2,1)} %bitcast.21, f32[256,2048]{1,0:T(8,128)} %compare_select_fusion), kind=kOutput, calls=%fused_computation.4 | convolution fusion | flops 1088421888 | bytes 7077888 | tf_op jit(solution)/shard_map/while/body/eval_jaxpr/hce,ehd->chd/dot_general | solution.py:75
  78.8 2.0 %copy.16 = f32[256,512]{1,0:T(8,128)} copy(f32[256,512]{0,1:T(8,128)} %bitcast.19) | data formatting | bytes 1048576 | tf_op jit(solution)/shard_map/reshape | solution.py:86
  80.8 0.0 reduce-scatter.2.cloned.1.call-update
  80.9 58.0 %reduce-scatter.2.cloned.1.call-done = f32[16,512]{1,0:T(8,128)} async-done(((f32[256,512]{1,0:T(8,128)}), f32[16,512]{1,0:T(8,128)}) %reduce-scatter.2.cloned.1.call-update) | async-done | bytes 32784 | tf_op jit(solution)/shard_map/reduce_scatter | solution.py:85
  138.8 0.9 reduce_sum.18
  139.7 0.9 multiply_reduce_fusion
  140.7 1.7 %fusion.1 = bf16[16,512]{1,0:T(8,128)(2,1)} fusion(bf16[512,512]{1,0:T(8,128)(2,1)S(1)} %copy-done.1, bf16[16,512]{1,0:T(8,128)(2,1)S(1)} %copy-done.3, f32[16,512]{1,0:T(8,128)} %reduce-scatter.2.cloned.1.call-done, f32[16]{0:T(128)S(1)} %add_sqrt_fusion, f32[16]{0:T(128)S(1)} %broadcast_multiply_fusion, bf16[512,512]{1,0:T(8,128)(2,1)S(1)} %copy-done.2), kind=kOutput, calls=%fused_computation.6 | convolution fusion | flops 16867328 | bytes 1114240 | tf_op jit(solution)/shard_map/dot_general | solution.py:96
  (47 shorter events, 0.2 us)
Async XLA Ops:
  6.5 48.1 %copy-start = (bf16[2048,512]{1,0:T(8,128)(2,1)S(1)}, bf16[2048,512]{1,0:T(8,128)(2,1)}, u32[]{:S(2)}) copy-start(bf16[2048,512]{1,0:T(8,128)(2,1)} %param.12) | copy-start | bytes 6291460
  6.5 48.1 %copy-start.4 = (bf16[512,512]{1,0:T(8,128)(2,1)S(1)}, bf16[512,512]{1,0:T(8,128)(2,1)}, u32[]{:S(2)}) copy-start(bf16[512,512]{1,0:T(8,128)(2,1)} %param.16) | copy-start | bytes 1572868
  6.5 132.3 %reduce-scatter.2.cloned.1.call-start = ((), (), s32[]{:S(2)}) async-start(), calls=%async_computation.1 | async-start | bytes 557056 | tf_op jit(solution)/shard_map/reduce_scatter | solution.py:85
  7.9 6.9 %collective-permute-start = (bf16[16,512]{1,0:T(8,128)(2,1)S(1)}, bf16[16,512]{1,0:T(8,128)(2,1)S(1)}, u32[]{:S(2)}, u32[]{:S(2)}) collective-permute-start(bf16[16,512]{1,0:T(8,128)(2,1)S(1)} %convolution_convert_fusion.2), channel_id=1, source_target_pairs={{0,1},{1,2},{2,3},{3,4},{4,5},{5,6},{6,7},{7,8},{8,9},{9,10},{10,1... | collective-permute-start | bytes 49160 | tf_op jit(solution)/shard_map/ppermute | solution.py:17
  14.8 5.9 %collective-permute-start.1 = (bf16[16,512]{1,0:T(8,128)(2,1)S(1)}, bf16[16,512]{1,0:T(8,128)(2,1)S(1)}, u32[]{:S(2)}, u32[]{:S(2)}) collective-permute-start(bf16[16,512]{1,0:T(8,128)(2,1)S(1)} %collective-permute-done), channel_id=1, source_target_pairs={{0,1},{1,2},{2,3},{3,4},{4,5},{5,6},{6,7},{7,8},{8,9},{9,10},{10,1... | collective-permute-start | bytes 49160 | tf_op jit(solution)/shard_map/ppermute | solution.py:17
  14.8 5.9 %collective-permute-start.8 = (bf16[16,512]{1,0:T(8,128)(2,1)S(1)}, bf16[16,512]{1,0:T(8,128)(2,1)S(1)}, u32[]{:S(2)}, u32[]{:S(2)}) collective-permute-start(bf16[16,512]{1,0:T(8,128)(2,1)S(1)} %convolution_convert_fusion.2), channel_id=1, source_target_pairs={{0,15},{1,0},{2,1},{3,2},{4,3},{5,4},{6,5},{7,6},{8,7},{9,8},{10,9... | collective-permute-start | bytes 49160 | tf_op jit(solution)/shard_map/ppermute | solution.py:19
  20.7 5.9 %collective-permute-start.2 = (bf16[16,512]{1,0:T(8,128)(2,1)S(1)}, bf16[16,512]{1,0:T(8,128)(2,1)S(1)}, u32[]{:S(2)}, u32[]{:S(2)}) collective-permute-start(bf16[16,512]{1,0:T(8,128)(2,1)S(1)} %collective-permute-done.1), channel_id=1, source_target_pairs={{0,1},{1,2},{2,3},{3,4},{4,5},{5,6},{6,7},{7,8},{8,9},{9,10},{10,1... | collective-permute-start | bytes 49160 | tf_op jit(solution)/shard_map/ppermute | solution.py:17
  20.7 5.9 %collective-permute-start.9 = (bf16[16,512]{1,0:T(8,128)(2,1)S(1)}, bf16[16,512]{1,0:T(8,128)(2,1)S(1)}, u32[]{:S(2)}, u32[]{:S(2)}) collective-permute-start(bf16[16,512]{1,0:T(8,128)(2,1)S(1)} %collective-permute-done.8), channel_id=1, source_target_pairs={{0,15},{1,0},{2,1},{3,2},{4,3},{5,4},{6,5},{7,6},{8,7},{9,8},{10,9... | collective-permute-start | bytes 49160 | tf_op jit(solution)/shard_map/ppermute | solution.py:19
  26.5 5.9 %collective-permute-start.3 = (bf16[16,512]{1,0:T(8,128)(2,1)S(1)}, bf16[16,512]{1,0:T(8,128)(2,1)S(1)}, u32[]{:S(2)}, u32[]{:S(2)}) collective-permute-start(bf16[16,512]{1,0:T(8,128)(2,1)S(1)} %collective-permute-done.2), channel_id=1, source_target_pairs={{0,1},{1,2},{2,3},{3,4},{4,5},{5,6},{6,7},{7,8},{8,9},{9,10},{10,1... | collective-permute-start | bytes 49160 | tf_op jit(solution)/shard_map/ppermute | solution.py:17
  26.5 21.4 %collective-permute-start.10 = (bf16[16,512]{1,0:T(8,128)(2,1)S(1)}, bf16[16,512]{1,0:T(8,128)(2,1)S(1)}, u32[]{:S(2)}, u32[]{:S(2)}) collective-permute-start(bf16[16,512]{1,0:T(8,128)(2,1)S(1)} %collective-permute-done.9), channel_id=1, source_target_pairs={{0,15},{1,0},{2,1},{3,2},{4,3},{5,4},{6,5},{7,6},{8,7},{9,8},{10,9... | collective-permute-start | bytes 49160 | tf_op jit(solution)/shard_map/ppermute | solution.py:19
  32.4 15.5 %collective-permute-start.4 = (bf16[16,512]{1,0:T(8,128)(2,1)S(1)}, bf16[16,512]{1,0:T(8,128)(2,1)S(1)}, u32[]{:S(2)}, u32[]{:S(2)}) collective-permute-start(bf16[16,512]{1,0:T(8,128)(2,1)S(1)} %collective-permute-done.3), channel_id=1, source_target_pairs={{0,1},{1,2},{2,3},{3,4},{4,5},{5,6},{6,7},{7,8},{8,9},{9,10},{10,1... | collective-permute-start | bytes 49160 | tf_op jit(solution)/shard_map/ppermute | solution.py:17
  47.9 2.7 %collective-permute-start.11 = (bf16[16,512]{1,0:T(8,128)(2,1)S(1)}, bf16[16,512]{1,0:T(8,128)(2,1)S(1)}, u32[]{:S(2)}, u32[]{:S(2)}) collective-permute-start(bf16[16,512]{1,0:T(8,128)(2,1)S(1)} %collective-permute-done.10), channel_id=1, source_target_pairs={{0,15},{1,0},{2,1},{3,2},{4,3},{5,4},{6,5},{7,6},{8,7},{9,8},{10,9... | collective-permute-start | bytes 49160 | tf_op jit(solution)/shard_map/ppermute | solution.py:19
  47.9 6.7 %collective-permute-start.5 = (bf16[16,512]{1,0:T(8,128)(2,1)S(1)}, bf16[16,512]{1,0:T(8,128)(2,1)S(1)}, u32[]{:S(2)}, u32[]{:S(2)}) collective-permute-start(bf16[16,512]{1,0:T(8,128)(2,1)S(1)} %collective-permute-done.4), channel_id=1, source_target_pairs={{0,1},{1,2},{2,3},{3,4},{4,5},{5,6},{6,7},{7,8},{8,9},{9,10},{10,1... | collective-permute-start | bytes 49160 | tf_op jit(solution)/shard_map/ppermute | solution.py:17
  50.7 11.1 %copy-start.5 = (bf16[512,512]{1,0:T(8,128)(2,1)S(1)}, bf16[512,512]{1,0:T(8,128)(2,1)}, u32[]{:S(2)}) copy-start(bf16[512,512]{1,0:T(8,128)(2,1)} %param.17) | copy-start | bytes 1572868
  50.7 6.6 %collective-permute-start.12 = (bf16[16,512]{1,0:T(8,128)(2,1)S(1)}, bf16[16,512]{1,0:T(8,128)(2,1)S(1)}, u32[]{:S(2)}, u32[]{:S(2)}) collective-permute-start(bf16[16,512]{1,0:T(8,128)(2,1)S(1)} %collective-permute-done.11), channel_id=1, source_target_pairs={{0,15},{1,0},{2,1},{3,2},{4,3},{5,4},{6,5},{7,6},{8,7},{9,8},{10,9... | collective-permute-start | bytes 49160 | tf_op jit(solution)/shard_map/ppermute | solution.py:19
  54.7 7.1 %collective-permute-start.6 = (bf16[16,512]{1,0:T(8,128)(2,1)S(1)}, bf16[16,512]{1,0:T(8,128)(2,1)S(1)}, u32[]{:S(2)}, u32[]{:S(2)}) collective-permute-start(bf16[16,512]{1,0:T(8,128)(2,1)S(1)} %collective-permute-done.5), channel_id=1, source_target_pairs={{0,1},{1,2},{2,3},{3,4},{4,5},{5,6},{6,7},{7,8},{8,9},{9,10},{10,1... | collective-permute-start | bytes 49160 | tf_op jit(solution)/shard_map/ppermute | solution.py:17
  57.3 7.1 %collective-permute-start.13 = (bf16[16,512]{1,0:T(8,128)(2,1)S(1)}, bf16[16,512]{1,0:T(8,128)(2,1)S(1)}, u32[]{:S(2)}, u32[]{:S(2)}) collective-permute-start(bf16[16,512]{1,0:T(8,128)(2,1)S(1)} %collective-permute-done.12), channel_id=1, source_target_pairs={{0,15},{1,0},{2,1},{3,2},{4,3},{5,4},{6,5},{7,6},{8,7},{9,8},{10,9... | collective-permute-start | bytes 49160 | tf_op jit(solution)/shard_map/ppermute | solution.py:19
  61.7 7.1 %collective-permute-start.7 = (bf16[16,512]{1,0:T(8,128)(2,1)S(1)}, bf16[16,512]{1,0:T(8,128)(2,1)S(1)}, u32[]{:S(2)}, u32[]{:S(2)}) collective-permute-start(bf16[16,512]{1,0:T(8,128)(2,1)S(1)} %collective-permute-done.6), channel_id=1, source_target_pairs={{0,1},{1,2},{2,3},{3,4},{4,5},{5,6},{6,7},{7,8},{8,9},{9,10},{10,1... | collective-permute-start | bytes 49160 | tf_op jit(solution)/shard_map/ppermute | solution.py:17
  64.4 5.9 %collective-permute-start.14 = (bf16[16,512]{1,0:T(8,128)(2,1)S(1)}, bf16[16,512]{1,0:T(8,128)(2,1)S(1)}, u32[]{:S(2)}, u32[]{:S(2)}) collective-permute-start(bf16[16,512]{1,0:T(8,128)(2,1)S(1)} %collective-permute-done.13), channel_id=1, source_target_pairs={{0,15},{1,0},{2,1},{3,2},{4,3},{5,4},{6,5},{7,6},{8,7},{9,8},{10,9... | collective-permute-start | bytes 49160 | tf_op jit(solution)/shard_map/ppermute | solution.py:19
  70.6 70.1 %copy-start.1 = (bf16[512,512]{1,0:T(8,128)(2,1)S(1)}, bf16[512,512]{1,0:T(8,128)(2,1)}, u32[]{:S(2)}) copy-start(bf16[512,512]{1,0:T(8,128)(2,1)} %param.19) | copy-start | bytes 1572868
  70.6 70.0 %copy-start.2 = (bf16[512,512]{1,0:T(8,128)(2,1)S(1)}, bf16[512,512]{1,0:T(8,128)(2,1)}, u32[]{:S(2)}) copy-start(bf16[512,512]{1,0:T(8,128)(2,1)} %param.18) | copy-start | bytes 1572868
  70.6 70.0 %copy-start.3 = (bf16[16,512]{1,0:T(8,128)(2,1)S(1)}, bf16[16,512]{1,0:T(8,128)(2,1)}, u32[]{:S(2)}) copy-start(bf16[16,512]{1,0:T(8,128)(2,1)} %param.10) | copy-start | bytes 49156
Sparse Core Ops, SparseCore 0:
  81.0 57.7 reduce-scatter.1
